TPU v7x, 32 devices: a whole 2x2x4 slice. The times are simulated.
32 devices in a mesh: group: 4 (over z), replica: 8 (over y, x, core).
Axes of the slice: x: 2, y: 2, z: 4, core: 2. Of those that a mesh axis runs over, the one named last changes fastest.
Arguments:
- layer_input: bfloat16 [8, 1024, 2560], P('replica', 'group')
- positions: int32 [8, 1024], P('replica', 'group'), may hold values from 0 to 543, as said below
- piece_starts: int32 [8, 2], P('replica'), may hold values from 0 to 768, as said below
- gain_attn: bfloat16 [2560], P('group'), may hold values from 0.5 to 1.5
- w_query: bfloat16 [2560, 2560], P('group'), may hold values from -0.125 to 0.125
- w_key: bfloat16 [2560, 640], P('group'), may hold values from -0.125 to 0.125
- w_value: bfloat16 [2560, 640], P('group'), may hold values from -0.125 to 0.125
- w_out: bfloat16 [2560, 2560], P('group'), may hold values from -2 to 2
- gain_mlp: bfloat16 [2560], P('group'), may hold values from 0.5 to 1.5
- w_gate: bfloat16 [2560, 7168], P('group'), may hold values from -0.125 to 0.125
- w_up: bfloat16 [2560, 7168], P('group'), may hold values from -0.125 to 0.125
- w_down: bfloat16 [2560, 7168], P('group'), may hold values from -0.0625 to 0.0625
- out_grad: bfloat16 [8, 1024, 2560], P('replica', 'group'), may hold values from -6 to 6
Outputs:
- layer_out: bfloat16 [8, 1024, 2560], P('replica', 'group')
- input_grad: float32 [8, 1024, 2560], P('replica', 'group')
- grad_norm_attn: float32 [2560], P(('group', 'replica'))
- grad_query: float32 [2560, 2560], P(('group', 'replica'))
- grad_key: float32 [2560, 640], P(('group', 'replica'))
- grad_value: float32 [2560, 640], P(('group', 'replica'))
- grad_out: float32 [2560, 2560], P(('group', 'replica'))
- grad_norm_mlp: float32 [2560], P(('group', 'replica'))
- grad_gate: float32 [2560, 7168], P(('group', 'replica'))
- grad_up: float32 [2560, 7168], P(('group', 'replica'))
- grad_down: float32 [2560, 7168], P(('group', 'replica'))
- stream_rms: float32 [8, 3], P('replica')
Inputs may be any that keep to these rules, and one draw needn't show every extreme that they name: `piece_starts`: each sequence holds two picture pieces of 256 tokens that start at multiples of 128, the second starting 256 or more tokens after the first, both ending inside the sequence. `positions`: outside picture pieces a token's position is one more than the previous token's; the j-th token of a piece whose first token has position p gets p + j // 16, and the token after the piece gets p + 16; a sequence's first token has position 0.
All inputs are finite; a program needn't handle non-finite values.
Results may differ from a plain program's by a relative error of at most 0.018.
Values may be sent and summed in bfloat16 or wider, within the bound.
No kernel may reach another device: no remote copies, remote signals or barrier semaphores. Data moves between devices by JAX's collectives and lax.ppermute only.
A program may use at most 384 MiB of HBM per device.

v0:
```python
import jax
import jax.numpy as jnp
from jax import lax
from jax.sharding import PartitionSpec as P

HEADS = 32
KV_HEADS = 8
HEAD_DIM = 80
PIECE = 256
epsilon = 1e-05
rope_base = 1000000.0


def rope_tables(places):
    halves = HEAD_DIM // 2
    frequency = rope_base ** (-(jnp.arange(halves, dtype=jnp.float32) * 2.0 / HEAD_DIM))
    angles = places.astype(jnp.float32)[..., None] * frequency
    angles = jnp.concatenate([angles, angles], axis=-1)
    return (jnp.cos(angles), jnp.sin(angles))


def rotate(values, cosine, sine):
    halves = HEAD_DIM // 2
    turned = jnp.concatenate([-values[..., halves:], values[..., :halves]], axis=-1)
    return values * cosine[:, :, None, :] + turned * sine[:, :, None, :]


def unrotate(grads, cosine, sine):
    halves = HEAD_DIM // 2
    shifted = grads * sine[:, :, None, :]
    turned = jnp.concatenate([shifted[..., halves:], -shifted[..., :halves]], axis=-1)
    return grads * cosine[:, :, None, :] + turned


def times_t(left, right):
    return lax.dot_general(
        left, right, (((1,), (1,)), ((), ())), preferred_element_type=jnp.float32
    )


def inner_t(left, right):
    return lax.dot_general(
        left, right, (((0,), (0,)), ((), ())), preferred_element_type=jnp.float32
    )


def inverse_rms(values):
    return lax.rsqrt(jnp.mean(values * values, axis=-1, keepdims=True) + epsilon)


def norm_back(grad_normed, source, inverse, gain_full):
    weighted = grad_normed * gain_full
    average = jnp.mean(weighted * source, axis=-1, keepdims=True)
    return inverse * weighted - source * (inverse * inverse * inverse) * average


def piece_index(starts, places):
    labels = jnp.zeros(places.shape, jnp.int32)
    for which in range(2):
        inside = (places >= starts[which]) & (places < starts[which] + PIECE)
        labels = jnp.where(inside, which + 1, labels)
    return labels


def shards(
    layer_input,
    positions,
    piece_starts,
    gain_attn,
    w_query,
    w_key,
    w_value,
    w_out,
    gain_mlp,
    w_gate,
    w_up,
    w_down,
    out_grad,
):
    sequences, block_size, model_width = layer_input.shape
    token_rows = sequences * block_size
    kv_width = KV_HEADS * HEAD_DIM
    repeats = HEADS // KV_HEADS
    scaling = HEAD_DIM ** (-0.5)
    full_len = block_size * lax.axis_size("group")
    source = layer_input.astype(jnp.float32).reshape(token_rows, model_width)
    inverse_one = inverse_rms(source)
    unit_one = source * inverse_one
    gain_piece = lax.all_gather(gain_attn, "group", axis=0, tiled=True)
    query_piece = lax.all_gather(w_query, "group", axis=0, tiled=True)
    key_piece = lax.all_gather(w_key, "group", axis=0, tiled=True)
    value_piece = lax.all_gather(w_value, "group", axis=0, tiled=True)
    out_piece = lax.all_gather(w_out, "group", axis=0, tiled=True)
    scaled = unit_one * gain_piece.astype(jnp.float32)
    scaled = scaled.astype(jnp.bfloat16)
    query = jnp.dot(scaled, query_piece, preferred_element_type=jnp.float32)
    keyed = jnp.dot(scaled, key_piece, preferred_element_type=jnp.float32)
    valued = jnp.dot(scaled, value_piece, preferred_element_type=jnp.float32)
    normed = scaled
    gains = gain_piece
    out_full = out_piece
    query_lin, key_lin, value_lin, normed_one, gain_one_low, out_full = (
        query,
        keyed,
        valued,
        normed,
        gains,
        out_full,
    )
    gain_one = gain_one_low.astype(jnp.float32)
    cosine, sine = rope_tables(positions)
    query_rot = rotate(
        query_lin.reshape(sequences, block_size, HEADS, HEAD_DIM), cosine, sine
    ).astype(jnp.bfloat16)
    key_rot = rotate(
        key_lin.reshape(sequences, block_size, KV_HEADS, HEAD_DIM), cosine, sine
    ).astype(jnp.bfloat16)
    key_rot = key_rot.reshape(sequences, block_size, kv_width)
    value_low = value_lin.astype(jnp.bfloat16).reshape(sequences, block_size, kv_width)
    key_all, value_all = (
        lax.all_gather(key_rot, "group", axis=1, tiled=True),
        lax.all_gather(value_low, "group", axis=1, tiled=True),
    )
    query_places = lax.axis_index("group") * block_size + jnp.arange(block_size, dtype=jnp.int32)
    key_places = jnp.arange(full_len, dtype=jnp.int32)

    def allowed_for(starts):
        query_labels = piece_index(starts, query_places)
        key_labels = piece_index(starts, key_places)
        causal = key_places[None, :] <= query_places[:, None]
        same_piece = (query_labels[:, None] == key_labels[None, :]) & (query_labels[:, None] > 0)
        return causal | same_piece

    def scores_of(query_seq, key_seq, starts):
        grouped = query_seq.reshape(block_size, KV_HEADS, repeats, HEAD_DIM)
        keys_grouped = key_seq.reshape(full_len, KV_HEADS, HEAD_DIM)
        raw = (
            jnp.einsum("qkrd,skd->krqs", grouped, keys_grouped, preferred_element_type=jnp.float32)
            * scaling
        )
        return jnp.where(allowed_for(starts)[None, None], raw, -1e30)

    def attend_one(packed):
        query_seq, key_seq, value_seq, starts = packed
        masked = scores_of(query_seq, key_seq, starts)
        highest_score = jnp.max(masked, axis=-1, keepdims=True)
        raised = jnp.exp(masked - highest_score)
        summed = jnp.sum(raised, axis=-1, keepdims=True)
        chances_low = (raised / summed).astype(jnp.bfloat16)
        values_grouped = value_seq.reshape(full_len, KV_HEADS, HEAD_DIM)
        mixed = jnp.einsum(
            "krqs,skd->qkrd", chances_low, values_grouped, preferred_element_type=jnp.float32
        )
        return (mixed.reshape(block_size, model_width), highest_score + jnp.log(summed))

    mixed_all, log_totals = lax.map(attend_one, (query_rot, key_all, value_all, piece_starts))
    mixed_low = mixed_all.reshape(token_rows, model_width).astype(jnp.bfloat16)
    middle = source + times_t(mixed_low, out_full)
    inverse_two = inverse_rms(middle)
    unit_two = middle * inverse_two
    gain_piece = lax.all_gather(gain_mlp, "group", axis=0, tiled=True)
    gate_piece = lax.all_gather(w_gate, "group", axis=0, tiled=True)
    up_piece = lax.all_gather(w_up, "group", axis=0, tiled=True)
    down_piece = lax.all_gather(w_down, "group", axis=0, tiled=True)
    scaled = unit_two * gain_piece.astype(jnp.float32)
    scaled = scaled.astype(jnp.bfloat16)
    gated = jnp.dot(scaled, gate_piece, preferred_element_type=jnp.float32)
    lifted = jnp.dot(scaled, up_piece, preferred_element_type=jnp.float32)
    normed = scaled
    gains = gain_piece
    down_full = down_piece
    gated, lifted, normed_two, gain_two_low, down_full = (gated, lifted, normed, gains, down_full)
    gain_two = gain_two_low.astype(jnp.float32)
    activated = jax.nn.silu(gated)
    hidden = (activated * lifted).astype(jnp.bfloat16)
    output_full = middle + times_t(hidden, down_full)
    grad_low = out_grad.reshape(token_rows, model_width)
    grad_top = grad_low.astype(jnp.float32)
    grad_hidden = jnp.dot(grad_low, down_full, preferred_element_type=jnp.float32)
    sigmoid_gate = jax.nn.sigmoid(gated)
    grad_gate_low = (
        grad_hidden * lifted * (sigmoid_gate + gated * sigmoid_gate * (1.0 - sigmoid_gate))
    ).astype(jnp.bfloat16)
    grad_lift_low = (grad_hidden * activated).astype(jnp.bfloat16)
    gate_piece = lax.all_gather(w_gate, "group", axis=0, tiled=True)
    up_piece = lax.all_gather(w_up, "group", axis=0, tiled=True)
    added = times_t(grad_gate_low, gate_piece) + times_t(grad_lift_low, up_piece)
    grad_normed_two = added
    grad_gain_two = jnp.sum(grad_normed_two * unit_two, axis=0)
    grad_middle = grad_top + norm_back(grad_normed_two, middle, inverse_two, gain_two)
    grad_middle_low = grad_middle.astype(jnp.bfloat16)
    grad_mixed_low = jnp.dot(grad_middle_low, out_full, preferred_element_type=jnp.float32).astype(
        jnp.bfloat16
    )

    def attend_back(packed):
        query_seq, key_seq, value_seq, starts, log_total, grad_seq = packed
        masked = scores_of(query_seq, key_seq, starts)
        chances = jnp.exp(masked - log_total)
        grad_grouped = grad_seq.reshape(block_size, KV_HEADS, repeats, HEAD_DIM)
        values_grouped = value_seq.reshape(full_len, KV_HEADS, HEAD_DIM)
        keys_grouped = key_seq.reshape(full_len, KV_HEADS, HEAD_DIM)
        query_grouped = query_seq.reshape(block_size, KV_HEADS, repeats, HEAD_DIM)
        grad_value_seq = jnp.einsum(
            "krqs,qkrd->skd",
            chances.astype(jnp.bfloat16),
            grad_grouped,
            preferred_element_type=jnp.float32,
        )
        grad_chance = jnp.einsum(
            "qkrd,skd->krqs", grad_grouped, values_grouped, preferred_element_type=jnp.float32
        )
        grad_score = chances * (
            grad_chance - jnp.sum(chances * grad_chance, axis=-1, keepdims=True)
        )
        grad_score = grad_score.astype(jnp.bfloat16)
        grad_query_seq = (
            jnp.einsum(
                "krqs,skd->qkrd", grad_score, keys_grouped, preferred_element_type=jnp.float32
            )
            * scaling
        )
        grad_key_seq = (
            jnp.einsum(
                "krqs,qkrd->skd", grad_score, query_grouped, preferred_element_type=jnp.float32
            )
            * scaling
        )
        return (
            grad_query_seq.reshape(block_size, HEADS, HEAD_DIM),
            grad_key_seq.reshape(full_len, kv_width),
            grad_value_seq.reshape(full_len, kv_width),
        )

    grad_query_rot, grad_key_full, grad_value_full = lax.map(
        attend_back,
        (
            query_rot,
            key_all,
            value_all,
            piece_starts,
            log_totals,
            grad_mixed_low.reshape(sequences, block_size, model_width),
        ),
    )
    grad_key_rot, grad_value_sum = (
        lax.psum_scatter(grad_key_full, "group", scatter_dimension=1, tiled=True),
        lax.psum_scatter(grad_value_full, "group", scatter_dimension=1, tiled=True),
    )
    grad_query_low = (
        unrotate(grad_query_rot, cosine, sine).astype(jnp.bfloat16).reshape(token_rows, model_width)
    )
    grad_key_low = (
        unrotate(grad_key_rot.reshape(sequences, block_size, KV_HEADS, HEAD_DIM), cosine, sine)
        .astype(jnp.bfloat16)
        .reshape(token_rows, kv_width)
    )
    grad_value_low = grad_value_sum.astype(jnp.bfloat16).reshape(token_rows, kv_width)
    query_piece = lax.all_gather(w_query, "group", axis=0, tiled=True)
    key_piece = lax.all_gather(w_key, "group", axis=0, tiled=True)
    value_piece = lax.all_gather(w_value, "group", axis=0, tiled=True)
    added = (
        times_t(grad_query_low, query_piece)
        + times_t(grad_key_low, key_piece)
        + times_t(grad_value_low, value_piece)
    )
    grad_gain_one = jnp.sum(added * unit_one, axis=0)
    input_grad = grad_middle + norm_back(added, source, inverse_one, gain_one)
    normed_own, middle_own, normed_mlp_own, top_own = (
        lax.all_to_all(normed_one, "group", split_axis=1, concat_axis=0, tiled=True),
        lax.all_to_all(grad_middle_low, "group", split_axis=1, concat_axis=0, tiled=True),
        lax.all_to_all(normed_two, "group", split_axis=1, concat_axis=0, tiled=True),
        lax.all_to_all(grad_low, "group", split_axis=1, concat_axis=0, tiled=True),
    )
    query_rows, key_rows, value_rows, mixed_rows = (
        lax.all_gather(grad_query_low, "group", axis=0, tiled=True),
        lax.all_gather(grad_key_low, "group", axis=0, tiled=True),
        lax.all_gather(grad_value_low, "group", axis=0, tiled=True),
        lax.all_gather(mixed_low, "group", axis=0, tiled=True),
    )
    gate_rows, lift_rows, hidden_rows = (
        lax.all_gather(grad_gate_low, "group", axis=0, tiled=True),
        lax.all_gather(grad_lift_low, "group", axis=0, tiled=True),
        lax.all_gather(hidden, "group", axis=0, tiled=True),
    )
    partial_sums = (
        inner_t(normed_own, query_rows),
        inner_t(normed_own, key_rows),
        inner_t(normed_own, value_rows),
        inner_t(middle_own, mixed_rows),
        inner_t(normed_mlp_own, gate_rows),
        inner_t(normed_mlp_own, lift_rows),
        inner_t(top_own, hidden_rows),
    )
    grad_query, grad_key, grad_value, grad_out, grad_gate, grad_up, grad_down = (
        lax.psum_scatter(
            partial_sums[0].astype(jnp.bfloat16), "replica", scatter_dimension=0, tiled=True
        ).astype(jnp.float32),
        lax.psum_scatter(
            partial_sums[1].astype(jnp.bfloat16), "replica", scatter_dimension=0, tiled=True
        ).astype(jnp.float32),
        lax.psum_scatter(
            partial_sums[2].astype(jnp.bfloat16), "replica", scatter_dimension=0, tiled=True
        ).astype(jnp.float32),
        lax.psum_scatter(
            partial_sums[3].astype(jnp.bfloat16), "replica", scatter_dimension=0, tiled=True
        ).astype(jnp.float32),
        lax.psum_scatter(
            partial_sums[4].astype(jnp.bfloat16), "replica", scatter_dimension=0, tiled=True
        ).astype(jnp.float32),
        lax.psum_scatter(
            partial_sums[5].astype(jnp.bfloat16), "replica", scatter_dimension=0, tiled=True
        ).astype(jnp.float32),
        lax.psum_scatter(
            partial_sums[6].astype(jnp.bfloat16), "replica", scatter_dimension=0, tiled=True
        ).astype(jnp.float32),
    )
    gain_owned = lax.psum_scatter(
        jnp.stack([grad_gain_one, grad_gain_two]),
        ("group", "replica"),
        scatter_dimension=1,
        tiled=True,
    )
    squares = jnp.stack(
        [
            jnp.sum((source * source).reshape(sequences, -1), axis=1),
            jnp.sum((middle * middle).reshape(sequences, -1), axis=1),
            jnp.sum((output_full * output_full).reshape(sequences, -1), axis=1),
        ],
        axis=1,
    )
    square_totals = lax.psum(squares, "group")
    stream_rms = jnp.sqrt(square_totals / (full_len * model_width))
    layer_out = output_full.astype(jnp.bfloat16).reshape(sequences, block_size, model_width)
    input_grad = input_grad.reshape(sequences, block_size, model_width)
    return (
        layer_out,
        input_grad,
        gain_owned[0],
        grad_query,
        grad_key,
        grad_value,
        grad_out,
        gain_owned[1],
        grad_gate,
        grad_up,
        grad_down,
        stream_rms,
    )


def solution(mesh):
    placed = (
        P("replica", "group", None),
        P("replica", "group"),
        P("replica", None),
        P("group"),
        P("group", None),
        P("group", None),
        P("group", None),
        P("group", None),
        P("group"),
        P("group", None),
        P("group", None),
        P("group", None),
        P("replica", "group", None),
    )
    return jax.shard_map(
        shards,
        mesh=mesh,
        in_specs=placed,
        out_specs=(
            P("replica", "group", None),
            P("replica", "group", None),
            P(("group", "replica")),
            P(("group", "replica"), None),
            P(("group", "replica"), None),
            P(("group", "replica"), None),
            P(("group", "replica"), None),
            P(("group", "replica")),
            P(("group", "replica"), None),
            P(("group", "replica"), None),
            P(("group", "replica"), None),
            P("replica", None),
        ),
        check_vma=False,
    )
```

profile of v0, /device:TPU:0, one launch (start us, length us, event | category | flops | bytes accessed | tf_op | source)
XLA Modules:
  0.0 4407.7 jit_solution(10174914001787924033)
XLA Ops:
  9.4 14.6 all-gather.3
  27.3 50.7 %all-gather.24.cloned.1.call-done = bf16[2560,640]{1,0:T(8,128)(2,1)} async-done(((bf16[640,640]{1,0:T(8,128)(2,1)}), bf16[2560,640]{1,0:T(8,128)(2,1)}) %all-gather.24.cloned.1.call-update) | async-done | bytes 3276816 | tf_op jit(solution)/shard_map/all_gather | solution.py:91
  78.0 4.0 fusion.41
  86.8 57.1 %all-gather.22.cloned.1.call-done = bf16[2560,640]{1,0:T(8,128)(2,1)} async-done(((bf16[640,640]{1,0:T(8,128)(2,1)}), bf16[2560,640]{1,0:T(8,128)(2,1)}) %all-gather.22.cloned.1.call-update) | async-done | bytes 3276816 | tf_op jit(solution)/shard_map/all_gather | solution.py:92
  143.9 3.9 convolution_convert_fusion.8
  153.2 13.6 all-gather.4
  169.8 7.8 all-gather.50.cloned.1.call-done
  179.2 32.1 all-gather.48.cloned.1.call-done
  213.7 224.8 %all-gather.26.cloned.1.call-done = bf16[2560,2560]{1,0:T(8,128)(2,1)} async-done(((bf16[640,2560]{1,0:T(8,128)(2,1)}), bf16[2560,2560]{1,0:T(8,128)(2,1)}) %all-gather.26.cloned.1.call-update) | async-done | bytes 13107216 | tf_op jit(solution)/shard_map/all_gather | solution.py:90
  438.5 8.5 fusion.39
  447.7 14.4 fusion.49
  462.2 13.2 fusion.3
  475.4 13.8 fusion.28
  489.3 175.7 %all-gather.28.cloned.1.call-done = bf16[2560,2560]{1,0:T(8,128)(2,1)} async-done(((bf16[640,2560]{1,0:T(8,128)(2,1)}), bf16[2560,2560]{1,0:T(8,128)(2,1)}) %all-gather.28.cloned.1.call-update) | async-done | bytes 13107216 | tf_op jit(solution)/shard_map/all_gather | solution.py:93
  664.9 7.0 multiply_reduce_fusion.4
  673.9 605.2 %all-gather.30.cloned.1.call-done = bf16[2560,7168]{1,0:T(8,128)(2,1)} async-done(((bf16[640,7168]{1,0:T(8,128)(2,1)}), bf16[2560,7168]{1,0:T(8,128)(2,1)}) %all-gather.30.cloned.1.call-update) | async-done | bytes 36700176 | tf_op jit(solution)/shard_map/all_gather | solution.py:162
  1279.1 24.5 fusion.50
  1303.6 590.1 %all-gather.32.cloned.1.call-done = bf16[2560,7168]{1,0:T(8,128)(2,1)} async-done(((bf16[640,7168]{1,0:T(8,128)(2,1)}), bf16[2560,7168]{1,0:T(8,128)(2,1)}) %all-gather.32.cloned.1.call-update) | async-done | bytes 36700176 | tf_op jit(solution)/shard_map/all_gather | solution.py:163
  1893.7 24.5 fusion.51
  1918.3 590.1 %all-gather.34.cloned.1.call-done = bf16[2560,7168]{1,0:T(8,128)(2,1)} async-done(((bf16[640,7168]{1,0:T(8,128)(2,1)}), bf16[2560,7168]{1,0:T(8,128)(2,1)}) %all-gather.34.cloned.1.call-update) | async-done | bytes 36700176 | tf_op jit(solution)/shard_map/all_gather | solution.py:164
  2508.4 27.7 multiply_convert_fusion
  2536.1 18.5 fusion.52
  2554.6 21.0 multiply_reduce_fusion.1
  2575.6 4.4 fusion.44
  2581.1 8.3 convolution_convert_fusion.5
  2590.0 14.7 fusion.5
  2606.1 22.3 fusion
  2628.4 28.1 fusion.2
  2656.5 12.5 bitcast_multiply_fusion.3
  2671.6 48.2 %reduce-scatter.15.cloned.1.call-done = f32[1,256,640]{1,2,0:T(8,128)} async-done(((f32[1,1024,640]{1,2,0:T(8,128)}), f32[1,256,640]{1,2,0:T(8,128)}) %reduce-scatter.15.cloned.1.call-update) | async-done | bytes 655376 | tf_op jit(solution)/shard_map/reduce_scatter | solution.py:247
  2722.5 9.0 convolution_multiply_fusion
  2737.5 4.3 all-to-all-start.1
  2741.9 6.9 fusion.53
  2751.2 3.1 fusion.18
  2756.1 91.9 %all-gather.40.cloned.1.call-done = bf16[1024,2560]{0,1:T(8,128)(2,1)} async-done(((bf16[256,2560]{0,1:T(8,128)(2,1)}), bf16[1024,2560]{0,1:T(8,128)(2,1)}) %all-gather.40.cloned.1.call-update) | async-done | bytes 5242896 | tf_op jit(solution)/shard_map/all_gather | solution.py:279
  2848.0 8.2 convolution_convert_fusion.3
  2861.0 51.0 %all_to_all.73 = bf16[256,4,640]{2,0,1:T(8,128)(2,1)S(1)} all-to-all(bf16[256,4,640]{2,0,1:T(8,128)(2,1)S(1)} %fusion.27), channel_id=1, replica_groups=mesh['group'=4,'replica'=8] {'group'}, dimensions={1} | all-to-all | bytes 2621440 | tf_op jit(solution)/shard_map/all_to_all | solution.py:270
  2912.0 3.5 convolution_convert_fusion.6
  2915.5 24.7 all-gather.38.cloned.1.call-done
  2940.3 3.4 convolution_convert_fusion.7
  2943.8 94.7 %all-gather.36.cloned.1.call-done = bf16[1024,2560]{0,1:T(8,128)(2,1)} async-done(((bf16[256,2560]{0,1:T(8,128)(2,1)}), bf16[1024,2560]{0,1:T(8,128)(2,1)}) %all-gather.36.cloned.1.call-update) | async-done | bytes 5242896 | tf_op jit(solution)/shard_map/all_gather | solution.py:276
  3038.5 7.8 convolution_convert_fusion.4
  3049.3 76.3 %all_to_all.74 = bf16[256,4,640]{0,2,1:T(8,128)(2,1)S(1)} all-to-all(bf16[256,4,640]{0,2,1:T(8,128)(2,1)} %bitcast.221), channel_id=1, replica_groups=mesh['group'=4,'replica'=8] {'group'}, dimensions={1} | all-to-all | bytes 2621440 | tf_op jit(solution)/shard_map/all_to_all | solution.py:273
  3127.0 191.6 %all-gather.46.cloned.1.call-done = bf16[1024,7168]{1,0:T(8,128)(2,1)} async-done(((bf16[256,7168]{1,0:T(8,128)(2,1)}), bf16[1024,7168]{1,0:T(8,128)(2,1)}) %all-gather.46.cloned.1.call-update) | async-done | bytes 14680080 | tf_op jit(solution)/shard_map/all_gather | solution.py:284
  3318.6 17.5 fusion.9
  3336.1 12.9 copy.109
  3350.5 75.0 %all_to_all.75 = bf16[256,4,640]{2,0,1:T(8,128)(2,1)S(1)} all-to-all(bf16[256,4,640]{2,0,1:T(8,128)(2,1)S(1)} %bitcast.220), channel_id=1, replica_groups=mesh['group'=4,'replica'=8] {'group'}, dimensions={1} | all-to-all | bytes 2621440 | tf_op jit(solution)/shard_map/all_to_all | solution.py:272
  3425.5 173.3 %all-gather.42.cloned.1.call-done = bf16[1024,7168]{1,0:T(8,128)(2,1)} async-done(((bf16[256,7168]{1,0:T(8,128)(2,1)}), bf16[1024,7168]{1,0:T(8,128)(2,1)}) %all-gather.42.cloned.1.call-update) | async-done | bytes 14680080 | tf_op jit(solution)/shard_map/all_gather | solution.py:282
  3598.7 17.4 convolution_convert_fusion.1
  3616.4 234.5 %all-gather.44.cloned.1.call-done = bf16[1024,7168]{1,0:T(8,128)(2,1)} async-done(((bf16[256,7168]{1,0:T(8,128)(2,1)}), bf16[1024,7168]{1,0:T(8,128)(2,1)}) %all-gather.44.cloned.1.call-update) | async-done | bytes 14680080 | tf_op jit(solution)/shard_map/all_gather | solution.py:283
  3850.8 17.4 convolution_convert_fusion
  3869.5 20.0 multiply_reduce_fusion
  3891.5 8.6 psum.7
  3900.7 4.8 fusion.24
  3905.4 81.6 %reduce-scatter.31.cloned.1.call-done = f32[80,2]{1,0:T(8,128)} async-done(((f32[2560,2]{1,0:T(8,128)}), f32[80,2]{1,0:T(8,128)}) %reduce-scatter.31.cloned.1.call-update) | async-done | bytes 656
  3989.1 44.5 %reduce-scatter.25.cloned.1.call-done = bf16[80,2560]{1,0:T(8,128)(2,1)} async-done(((bf16[640,2560]{1,0:T(8,128)(2,1)}), bf16[80,2560]{1,0:T(8,128)(2,1)}) %reduce-scatter.25.cloned.1.call-update) | async-done | bytes 409616 | tf_op jit(solution)/shard_map/reduce_scatter | solution.py:305
  4035.5 36.8 reduce-scatter.23.cloned.1.call-done
  4073.9 36.8 reduce-scatter.21.cloned.1.call-done
  4112.4 49.1 %reduce-scatter.19.cloned.1.call-done = bf16[80,2560]{1,0:T(8,128)(2,1)} async-done(((bf16[640,2560]{1,0:T(8,128)(2,1)}), bf16[80,2560]{1,0:T(8,128)(2,1)}) %reduce-scatter.19.cloned.1.call-update) | async-done | bytes 409616 | tf_op jit(solution)/shard_map/reduce_scatter | solution.py:296
  4163.4 77.1 %reduce-scatter.33.cloned.1.call-done = bf16[80,7168]{1,0:T(8,128)(2,1)} async-done(((bf16[640,7168]{1,0:T(8,128)(2,1)}), bf16[80,7168]{1,0:T(8,128)(2,1)}) %reduce-scatter.33.cloned.1.call-update) | async-done | bytes 1146896
  4244.3 74.9 %reduce-scatter.27.cloned.1.call-done = bf16[80,7168]{1,0:T(8,128)(2,1)} async-done(((bf16[640,7168]{1,0:T(8,128)(2,1)}), bf16[80,7168]{1,0:T(8,128)(2,1)}) %reduce-scatter.27.cloned.1.call-update) | async-done | bytes 1146896 | tf_op jit(solution)/shard_map/reduce_scatter | solution.py:308
  4319.2 2.8 convert_element_type.179
  4322.0 76.2 %reduce-scatter.29.cloned.1.call-done = bf16[80,7168]{1,0:T(8,128)(2,1)} async-done(((bf16[640,7168]{1,0:T(8,128)(2,1)}), bf16[80,7168]{1,0:T(8,128)(2,1)}) %reduce-scatter.29.cloned.1.call-update) | async-done | bytes 1146896 | tf_op jit(solution)/shard_map/reduce_scatter | solution.py:311
  4398.2 2.8 convert_element_type.181
  (196 shorter events, 69.7 us)
Async XLA Ops:
  7.2 70.8 %all-gather.24.cloned.1.call-start = ((), (), s32[]{:S(2)}) async-start(), calls=%async_computation.15 | async-start | bytes 4096000 | tf_op jit(solution)/shard_map/all_gather | solution.py:91
  7.9 18.5 copy-start
  7.9 135.9 %all-gather.22.cloned.1.call-start = ((), (), s32[]{:S(2)}) async-start(), calls=%async_computation.14 | async-start | bytes 4096000 | tf_op jit(solution)/shard_map/all_gather | solution.py:92
  8.7 168.9 %all-gather.50.cloned.1.call-start = ((), (), s32[]{:S(2)}) async-start(), calls=%async_computation.36 | async-start | bytes 1638400 | tf_op jit(solution)/shard_map/all_gather | solution.py:121
  24.0 0.6 copy-start.29
  24.7 413.8 %copy-start.27 = (f32[2560]{0:T(1024)}, f32[2560]{0:T(1024)S(1)}, u32[]{:S(2)}) copy-start(f32[2560]{0:T(1024)S(1)} %reshape.535) | copy-start | bytes 30724
  25.8 421.4 %copy-start.22 = (f32[256,80]{0,1:T(8,128)}, f32[256,80]{0,1:T(8,128)S(1)}, u32[]{:S(2)}) copy-start(f32[256,80]{0,1:T(8,128)S(1)} %get-tuple-element.147) | copy-start | bytes 245764
  25.8 421.4 %copy-start.24 = (f32[256,80]{0,1:T(8,128)}, f32[256,80]{0,1:T(8,128)S(1)}, u32[]{:S(2)}) copy-start(f32[256,80]{0,1:T(8,128)S(1)} %get-tuple-element.148) | copy-start | bytes 245764
  27.3 411.2 %copy-start.31 = (f32[256]{0:T(256)}, f32[256]{0:T(256)S(1)}, u32[]{:S(2)}) copy-start(f32[256]{0:T(256)S(1)} %get-tuple-element.150) | copy-start | bytes 3076
  86.8 124.5 %all-gather.48.cloned.1.call-start = ((), (), s32[]{:S(2)}) async-start(), calls=%async_computation.35 | async-start | bytes 1638400 | tf_op jit(solution)/shard_map/all_gather | solution.py:122
  147.8 290.7 %all-gather.26.cloned.1.call-start = ((), (), s32[]{:S(2)}) async-start(), calls=%async_computation.16 | async-start | bytes 16384000 | tf_op jit(solution)/shard_map/all_gather | solution.py:90
  148.4 516.5 %all-gather.28.cloned.1.call-start = ((), (), s32[]{:S(2)}) async-start(), calls=%async_computation.17 | async-start | bytes 16384000 | tf_op jit(solution)/shard_map/all_gather | solution.py:93
  149.0 1130.1 %all-gather.30.cloned.1.call-start = ((), (), s32[]{:S(2)}) async-start(), calls=%async_computation.18 | async-start | bytes 45875200 | tf_op jit(solution)/shard_map/all_gather | solution.py:162
  149.7 1744.0 %all-gather.32.cloned.1.call-start = ((), (), s32[]{:S(2)}) async-start(), calls=%async_computation.19 | async-start | bytes 45875200 | tf_op jit(solution)/shard_map/all_gather | solution.py:163
  150.5 0.8 copy-start.35
  150.5 2.7 copy-start.34
  150.5 2357.9 %all-gather.34.cloned.1.call-start = ((), (), s32[]{:S(2)}) async-start(), calls=%async_computation.20 | async-start | bytes 45875200 | tf_op jit(solution)/shard_map/all_gather | solution.py:164
  151.2 2518.5 %reduce-scatter.17.cloned.1.call-start = ((), (), s32[]{:S(2)}) async-start(), calls=%async_computation.22 | async-start | bytes 3276800 | tf_op jit(solution)/shard_map/reduce_scatter | solution.py:248
  179.2 268.6 %copy-start.4 = (bf16[1024,640]{0,1:T(8,128)(2,1)}, bf16[1024,640]{0,1:T(8,128)(2,1)S(1)}, u32[]{:S(2)}) copy-start(bf16[1024,640]{0,1:T(8,128)(2,1)S(1)} %copy.84) | copy-start | bytes 3932164
  447.7 14.4 copy-start.2
  462.1 13.3 copy-start.8
  489.2 182.7 %copy-start.26 = (bf16[8,80,4,256]{3,1,2,0:T(8,128)(2,1)}, bf16[8,80,4,256]{3,1,2,0:T(8,128)(2,1)S(1)}, u32[]{:S(2)}) copy-start(bf16[8,80,4,256]{3,1,2,0:T(8,128)(2,1)S(1)} %fusion.28) | copy-start | bytes 3932164
  672.0 1.6 copy-start.6
  673.9 1219.8 %copy-start.12 = (bf16[256,2560]{1,0:T(8,128)(2,1)}, bf16[256,2560]{1,0:T(8,128)(2,1)S(1)}, u32[]{:S(2)}) copy-start(bf16[256,2560]{1,0:T(8,128)(2,1)S(1)} %multiply_convert_fusion.3) | copy-start | bytes 3932164
  1303.6 1204.8 %copy-start.10 = (bf16[1,256,2560]{2,1,0:T(8,128)(2,1)S(1)}, bf16[1,256,2560]{2,1,0:T(8,128)(2,1)}, u32[]{:S(2)}) copy-start(bf16[1,256,2560]{2,1,0:T(8,128)(2,1)} %param.25) | copy-start | bytes 3932164
  2536.1 18.5 copy-start.7
  2580.0 1.1 copy-start.14
  2604.7 1.3 copy-start.9
  2604.8 115.0 %reduce-scatter.15.cloned.1.call-start = ((), (), s32[]{:S(2)}) async-start(), calls=%async_computation.21 | async-start | bytes 3276800 | tf_op jit(solution)/shard_map/reduce_scatter | solution.py:247
  2628.4 28.1 copy-start.3
  2669.0 50.8 %copy-start.25 = (f32[256,80]{0,1:T(8,128)S(1)}, f32[256,80]{0,1:T(8,128)}, u32[]{:S(2)}) copy-start(f32[256,80]{0,1:T(8,128)} %copy-done.24) | copy-start | bytes 245764
  2669.0 178.9 %all-gather.40.cloned.1.call-start = ((), (), s32[]{:S(2)}) async-start(), calls=%async_computation.28 | async-start | bytes 6553600 | tf_op jit(solution)/shard_map/all_gather | solution.py:279
  2669.6 51.5 %copy-start.23 = (f32[256,80]{0,1:T(8,128)S(1)}, f32[256,80]{0,1:T(8,128)}, u32[]{:S(2)}) copy-start(f32[256,80]{0,1:T(8,128)} %copy-done.22) | copy-start | bytes 245764
  2669.6 242.4 %all-gather.52.cloned.1.call-start = ((), (), s32[]{:S(2)}) async-start(), calls=%async_computation.37 | async-start | bytes 1638400 | tf_op jit(solution)/shard_map/all_gather | solution.py:278
  2671.6 268.7 %all-gather.38.cloned.1.call-start = ((), (), s32[]{:S(2)}) async-start(), calls=%async_computation.25 | async-start | bytes 1638400 | tf_op jit(solution)/shard_map/all_gather | solution.py:277
  2719.8 1.4 copy-start.21
  2721.0 1.5 copy-start.5
  2722.0 316.5 %all-gather.36.cloned.1.call-start = ((), (), s32[]{:S(2)}) async-start(), calls=%async_computation.23 | async-start | bytes 6553600 | tf_op jit(solution)/shard_map/all_gather | solution.py:276
  2733.8 584.8 %all-gather.46.cloned.1.call-start = ((), (), s32[]{:S(2)}) async-start(), calls=%async_computation.34 | async-start | bytes 18350080 | tf_op jit(solution)/shard_map/all_gather | solution.py:284
  2734.4 864.3 %all-gather.42.cloned.1.call-start = ((), (), s32[]{:S(2)}) async-start(), calls=%async_computation.30 | async-start | bytes 18350080 | tf_op jit(solution)/shard_map/all_gather | solution.py:282
  2735.0 1.3 copy-start.15
  2735.0 1115.8 %all-gather.44.cloned.1.call-start = ((), (), s32[]{:S(2)}) async-start(), calls=%async_computation.32 | async-start | bytes 18350080 | tf_op jit(solution)/shard_map/all_gather | solution.py:283
  2736.3 5.6 copy-start.16
  2737.5 110.5 %all-to-all-start.1 = ((bf16[256,4,640]{2,0,1:T(8,128)(2,1)}), bf16[256,4,640]{2,0,1:T(8,128)(2,1)}, u32[]{:S(2)}, u32[]{:S(2)}) async-start(bf16[256,4,640]{2,0,1:T(8,128)(2,1)} %bitcast.218), calls=%async_computation.6 | async-start | bytes 2621440 | tf_op jit(solution)/shard_map/all_to_all | solution.py:271
  2741.8 7.0 copy-start.20
  2741.8 1245.2 %reduce-scatter.31.cloned.1.call-start = ((), (), s32[]{:S(2)}) async-start(), calls=%async_computation.38 | async-start | bytes 1351680
  2741.9 6.9 copy-start.17
  2748.8 1.3 copy-start.1
  2748.8 2.3 copy-start.18
  2748.8 2.3 copy-start.19
  2748.8 2.3 copy-start.28
  2748.9 2.3 copy-start.32
  2755.8 1277.8 %reduce-scatter.25.cloned.1.call-start = ((), (), s32[]{:S(2)}) async-start(), calls=%async_computation.29 | async-start | bytes 3686400 | tf_op jit(solution)/shard_map/reduce_scatter | solution.py:305
  2856.2 0.7 copy-start.30
  2856.2 1216.2 %reduce-scatter.23.cloned.1.call-start = ((), (), s32[]{:S(2)}) async-start(), calls=%async_computation.27 | async-start | bytes 921600 | tf_op jit(solution)/shard_map/reduce_scatter | solution.py:302
  2915.5 1195.3 %reduce-scatter.21.cloned.1.call-start = ((), (), s32[]{:S(2)}) async-start(), calls=%async_computation.26 | async-start | bytes 921600 | tf_op jit(solution)/shard_map/reduce_scatter | solution.py:299
  2943.7 1217.8 %reduce-scatter.19.cloned.1.call-start = ((), (), s32[]{:S(2)}) async-start(), calls=%async_computation.24 | async-start | bytes 3686400 | tf_op jit(solution)/shard_map/reduce_scatter | solution.py:296
  3046.4 1.6 copy-start.11
  3046.4 1194.1 %reduce-scatter.33.cloned.1.call-start = ((), (), s32[]{:S(2)}) async-start(), calls=%async_computation.39 | async-start | bytes 10321920
  3349.0 1.3 copy-start.13
  3349.1 970.1 %reduce-scatter.27.cloned.1.call-start = ((), (), s32[]{:S(2)}) async-start(), calls=%async_computation.31 | async-start | bytes 10321920 | tf_op jit(solution)/shard_map/reduce_scatter | solution.py:308
  3616.1 782.0 %reduce-scatter.29.cloned.1.call-start = ((), (), s32[]{:S(2)}) async-start(), calls=%async_computation.33 | async-start | bytes 10321920 | tf_op jit(solution)/shard_map/reduce_scatter | solution.py:311
  3869.5 31.1 copy-start.33
Sparse Core Ops, SparseCore 0:
  9.6 68.3 all-gather.23
  79.5 64.2 all-gather.21
  146.0 31.4 all-gather.49
  179.5 31.6 all-gather.47
  212.7 225.7 all-gather.25
  439.9 224.9 all-gather.27
  666.5 612.5 all-gather.29
  1280.6 613.0 all-gather.31
  1895.3 613.0 all-gather.33
  2604.9 50.8 reduce-scatter.16
  2669.2 50.5 reduce-scatter.14
  2721.2 126.6 all-gather.39
  2850.1 56.3 all-gather.51
  2908.5 31.7 all-gather.37
  2942.2 96.2 all-gather.35
  3039.9 278.6 all-gather.45
  3320.1 278.6 all-gather.41
  3600.2 250.6 all-gather.43
  3853.6 133.3 reduce-scatter.30
  3990.7 42.8 reduce-scatter.24
  4037.8 34.4 reduce-scatter.22
  4076.3 34.4 reduce-scatter.20
  4114.6 46.8 reduce-scatter.18
  4165.4 75.0 reduce-scatter.32
  4244.1 75.0 reduce-scatter.26
  4323.1 75.0 reduce-scatter.28
where the time goes:
time: 4410 us
  waiting for transfers between devices  3680 us (83%)
  matrix products  341 us (8%)
  blocking collectives  239 us (5%)
  other arithmetic  83.8 us (2%)
  local copies, waits for them, and re-layouts  45.3 us (1%)
    all_gather x1, waiting for transfers between devices, shards(): gate_piece = lax.all_gather(w_gate, 'group', axis=0, tiled=True)  605 us
    all_gather x1, waiting for transfers between devices, shards(): down_piece = lax.all_gather(w_down, 'group', axis=0, tiled=True)  590 us
    all_gather x1, waiting for transfers between devices, shards(): up_piece = lax.all_gather(w_up, 'group', axis=0, tiled=True)  590 us
    all_gather x1, waiting for transfers between devices, shards(): lax.all_gather(grad_lift_low, 'group', axis=0, tiled=True)  234 us
    all_gather x1, waiting for transfers between devices, shards(): query_piece = lax.all_gather(w_query, 'group', axis=0, tiled=True)  225 us
    all_gather x1, waiting for transfers between devices, shards(): lax.all_gather(hidden, 'group', axis=0, tiled=True)  192 us
    all_gather x1, waiting for transfers between devices, shards(): out_piece = lax.all_gather(w_out, 'group', axis=0, tiled=True)  176 us
    all_gather x1, waiting for transfers between devices, shards(): lax.all_gather(grad_gate_low, 'group', axis=0, tiled=True)  173 us
  transfers between devices with their start and end apart: 27, of which 24 were waited for; matrix products, arithmetic and copies ran while one was open for 8% of the time, Pallas kernels for 0%

commit v1 on v0

--- a/solution.py
+++ b/solution.py
@@ -159,7 +159,14 @@
     inverse_two = inverse_rms(middle)
     unit_two = middle * inverse_two
     gain_piece = lax.all_gather(gain_mlp, "group", axis=0, tiled=True)
-    gate_piece = lax.all_gather(w_gate, "group", axis=0, tiled=True)
+    ring = [w_gate]
+    for hop in range(3):
+        ring.append(lax.ppermute(ring[-1], "group", [(dev, (dev + 1) % 4) for dev in range(4)]))
+    gate_piece = jnp.roll(
+        jnp.concatenate(ring[::-1], axis=0),
+        (lax.axis_index("group") + 1) * ring[0].shape[0],
+        axis=0,
+    )
     up_piece = lax.all_gather(w_up, "group", axis=0, tiled=True)
     down_piece = lax.all_gather(w_down, "group", axis=0, tiled=True)
     scaled = unit_two * gain_piece.astype(jnp.float32)

time: 4410 us -> 4920 us (1.12)
  blocking collectives: 239 us -> 639 us
  starting transfers between devices: 5.94 us -> 88.2 us
  local copies, waits for them, and re-layouts: 45.3 us -> 108 us
    ppermute x0 -> x3, waiting for transfers between devices: none -> 697 us  [shards(): lax.ppermute(ring[-1], 'group', [(dev, (dev + 1) % 4) for dev in range(4)])]
    all_gather x1, blocking collectives: 13.6 us -> 414 us  [shards(): gain_piece = lax.all_gather(gain_mlp, 'group', axis=0, tiled=True)]
    all_gather x1, waiting for transfers between devices: 590 us -> 336 us  [shards(): up_piece = lax.all_gather(w_up, 'group', axis=0, tiled=True)]
    all_gather x1, waiting for transfers between devices: 225 us -> 0.01 us  [shards(): query_piece = lax.all_gather(w_query, 'group', axis=0, tiled=True)]
    all_gather x1, waiting for transfers between devices: 176 us -> 0.02 us  [shards(): out_piece = lax.all_gather(w_out, 'group', axis=0, tiled=True)]
    ppermute x0 -> x3, starting transfers between devices: none -> 82.4 us  [shards(): lax.ppermute(ring[-1], 'group', [(dev, (dev + 1) % 4) for dev in range(4)])]
    unnamed x82 -> x93, local copies, waits for them, and re-layouts: 31.5 us -> 84.8 us
  transfers between devices with their start and end apart: 27 -> 30, of which waited for: 24 -> 22; matrix products, arithmetic and copies ran while one was open for 8% -> 9% of each run, Pallas kernels for 0% -> 0%
where the time goes in v1:
time: 4920 us
  waiting for transfers between devices  3640 us (74%)
  blocking collectives  639 us (13%)
  matrix products  343 us (7%)
  local copies, waits for them, and re-layouts  108 us (2%)
  starting transfers between devices  88.2 us (2%)
  other arithmetic  85.3 us (2%)
    ppermute x3, waiting for transfers between devices, shards(): lax.ppermute(ring[-1], 'group', [(dev, (dev + 1) % 4) for dev in range(4)])  697 us
    all_gather x1, waiting for transfers between devices, shards(): down_piece = lax.all_gather(w_down, 'group', axis=0, tiled=True)  590 us
    all_gather x1, waiting for transfers between devices, shards(): gate_piece = lax.all_gather(w_gate, 'group', axis=0, tiled=True)  562 us
    all_gather x1, blocking collectives, shards(): gain_piece = lax.all_gather(gain_mlp, 'group', axis=0, tiled=True)  414 us
    all_gather x1, waiting for transfers between devices, shards(): up_piece = lax.all_gather(w_up, 'group', axis=0, tiled=True)  336 us
    all_gather x1, waiting for transfers between devices, shards(): lax.all_gather(grad_lift_low, 'group', axis=0, tiled=True)  234 us
    all_gather x1, waiting for transfers between devices, shards(): lax.all_gather(hidden, 'group', axis=0, tiled=True)  192 us
    all_gather x1, waiting for transfers between devices, shards(): lax.all_gather(grad_gate_low, 'group', axis=0, tiled=True)  173 us
  transfers between devices with their start and end apart: 30, of which 22 were waited for; matrix products, arithmetic and copies ran while one was open for 9% of the time, Pallas kernels for 0%

profile of v1, /device:TPU:0, one launch (start us, length us, event | category | flops | bytes accessed | tf_op | source)
XLA Modules:
  0.0 4915.6 jit_solution(17902910795167082891)
XLA Ops:
  9.4 14.6 all-gather.3
  27.3 50.6 %all-gather.24.cloned.1.call-done = bf16[2560,640]{1,0:T(8,128)(2,1)} async-done(((bf16[640,640]{1,0:T(8,128)(2,1)}), bf16[2560,640]{1,0:T(8,128)(2,1)}) %all-gather.24.cloned.1.call-update) | async-done | bytes 3276816 | tf_op jit(solution)/shard_map/all_gather | solution.py:91
  86.8 57.1 %all-gather.22.cloned.1.call-done = bf16[2560,640]{1,0:T(8,128)(2,1)} async-done(((bf16[640,640]{1,0:T(8,128)(2,1)}), bf16[2560,640]{1,0:T(8,128)(2,1)}) %all-gather.22.cloned.1.call-update) | async-done | bytes 3276816 | tf_op jit(solution)/shard_map/all_gather | solution.py:92
  151.3 369.6 %collective-permute-done = bf16[640,7168]{1,0:T(8,128)(2,1)} collective-permute-done((bf16[640,7168]{1,0:T(8,128)(2,1)}, bf16[640,7168]{1,0:T(8,128)(2,1)}, u32[]{:S(2)}, u32[]{:S(2)}) %collective-permute-start) | collective-permute-done | bytes 9175072 | tf_op jit(solution)/shard_map/ppermute | solution.py:164
  521.0 81.6 %collective-permute-start.1 = (bf16[640,7168]{1,0:T(8,128)(2,1)}, bf16[640,7168]{1,0:T(8,128)(2,1)}, u32[]{:S(2)}, u32[]{:S(2)}) collective-permute-start(bf16[640,7168]{1,0:T(8,128)(2,1)} %collective-permute-done), channel_id=1, source_target_pairs={{0,8},{8,16},{16,24},{24,0},{1,9},{9,17},{17,25},{25,1},{2,10},{10... | collective-permute-start | bytes 27525128 | tf_op jit(solution)/shard_map/ppermute | solution.py:164
  604.5 413.9 %all-gather.4 = bf16[4,1,640]{2,1,0:T(2,128)(2,1)S(1)} all-gather(bf16[1,1,640]{2,1,0:T(2,128)(2,1)S(1)} %reshape.533), channel_id=1, replica_groups=mesh['group'=4,'replica'=8] {'group'}, dimensions={0}, use_global_device_ids=true | all-gather | bytes 6400 | tf_op jit(solution)/shard_map/all_gather | solution.py:161
  1027.5 9.8 fusion.42
  1038.1 14.4 fusion.52
  1052.5 13.1 fusion.5
  1065.6 13.7 fusion.30
  1079.4 7.7 multiply_reduce_fusion.4
  1088.9 327.2 %collective-permute-done.2 = bf16[640,7168]{1,0:T(8,128)(2,1)} collective-permute-done((bf16[640,7168]{1,0:T(8,128)(2,1)}, bf16[640,7168]{1,0:T(8,128)(2,1)}, u32[]{:S(2)}, u32[]{:S(2)}) %collective-permute-start.2) | collective-permute-done | bytes 9175072 | tf_op jit(solution)/shard_map/ppermute | solution.py:164
  1416.2 7.8 constant_dynamic-update-slice_fusion.7
  1423.9 7.8 constant_dynamic-update-slice_fusion.6
  1431.8 7.9 constant_dynamic-update-slice_fusion.5
  1439.7 7.8 constant_dynamic-update-slice_fusion.4
  1447.4 7.8 constant_dynamic-update-slice_fusion.3
  1455.2 7.8 constant_dynamic-update-slice_fusion.2
  1463.0 7.8 constant_dynamic-update-slice_fusion.1
  1470.8 7.8 constant_dynamic-update-slice_fusion
  1478.6 335.8 %all-gather.30.cloned.1.call-done = bf16[2560,7168]{1,0:T(8,128)(2,1)} async-done(((bf16[640,7168]{1,0:T(8,128)(2,1)}), bf16[2560,7168]{1,0:T(8,128)(2,1)}) %all-gather.30.cloned.1.call-update) | async-done | bytes 36700176 | tf_op jit(solution)/shard_map/all_gather | solution.py:170
  1814.4 24.7 fusion.53
  1839.1 589.8 %all-gather.32.cloned.1.call-done = bf16[2560,7168]{1,0:T(8,128)(2,1)} async-done(((bf16[640,7168]{1,0:T(8,128)(2,1)}), bf16[2560,7168]{1,0:T(8,128)(2,1)}) %all-gather.32.cloned.1.call-update) | async-done | bytes 36700176 | tf_op jit(solution)/shard_map/all_gather | solution.py:171
  2428.9 24.8 fusion.32
  2453.7 27.5 multiply_convert_fusion
  2481.2 562.4 %all-gather.34.cloned.1.call-done = bf16[2560,7168]{1,0:T(8,128)(2,1)} async-done(((bf16[640,7168]{1,0:T(8,128)(2,1)}), bf16[2560,7168]{1,0:T(8,128)(2,1)}) %all-gather.34.cloned.1.call-update) | async-done | bytes 36700176 | tf_op jit(solution)/shard_map/all_gather | solution.py:192
  3043.6 18.5 fusion.54
  3062.1 20.8 multiply_reduce_fusion.1
  3082.9 4.5 fusion.47
  3088.5 8.3 convolution_convert_fusion.5
  3097.5 14.8 fusion.7
  3113.6 22.8 fusion.2
  3136.4 28.1 fusion.4
  3164.5 12.4 bitcast_multiply_fusion.3
  3179.5 48.2 reduce-scatter.15.cloned.1.call-done
  3230.4 9.1 convolution_multiply_fusion
  3245.4 4.3 all-to-all-start.1
  3249.8 7.0 fusion.55
  3263.9 91.9 %all-gather.40.cloned.1.call-done = bf16[1024,2560]{0,1:T(8,128)(2,1)} async-done(((bf16[256,2560]{0,1:T(8,128)(2,1)}), bf16[1024,2560]{0,1:T(8,128)(2,1)}) %all-gather.40.cloned.1.call-update) | async-done | bytes 5242896 | tf_op jit(solution)/shard_map/all_gather | solution.py:286
  3355.9 8.2 convolution_convert_fusion.3
  3368.8 50.8 %all_to_all.73 = bf16[256,4,640]{2,0,1:T(8,128)(2,1)S(1)} all-to-all(bf16[256,4,640]{2,0,1:T(8,128)(2,1)S(1)} %fusion.29), channel_id=1, replica_groups=mesh['group'=4,'replica'=8] {'group'}, dimensions={1} | all-to-all | bytes 2621440 | tf_op jit(solution)/shard_map/all_to_all | solution.py:277
  3423.4 24.5 all-gather.38.cloned.1.call-done
  3451.4 94.7 %all-gather.36.cloned.1.call-done = bf16[1024,2560]{0,1:T(8,128)(2,1)} async-done(((bf16[256,2560]{0,1:T(8,128)(2,1)}), bf16[1024,2560]{0,1:T(8,128)(2,1)}) %all-gather.36.cloned.1.call-update) | async-done | bytes 5242896 | tf_op jit(solution)/shard_map/all_gather | solution.py:283
  3546.2 7.8 convolution_convert_fusion.4
  3556.9 76.4 %all_to_all.74 = bf16[256,4,640]{0,2,1:T(8,128)(2,1)S(1)} all-to-all(bf16[256,4,640]{0,2,1:T(8,128)(2,1)} %bitcast.218), channel_id=1, replica_groups=mesh['group'=4,'replica'=8] {'group'}, dimensions={1} | all-to-all | bytes 2621440 | tf_op jit(solution)/shard_map/all_to_all | solution.py:280
  3634.7 191.6 %all-gather.46.cloned.1.call-done = bf16[1024,7168]{1,0:T(8,128)(2,1)} async-done(((bf16[256,7168]{1,0:T(8,128)(2,1)}), bf16[1024,7168]{1,0:T(8,128)(2,1)}) %all-gather.46.cloned.1.call-update) | async-done | bytes 14680080 | tf_op jit(solution)/shard_map/all_gather | solution.py:291
  3826.3 17.4 fusion.11
  3843.7 12.9 copy.109
  3858.1 75.1 %all_to_all.75 = bf16[256,4,640]{2,0,1:T(8,128)(2,1)S(1)} all-to-all(bf16[256,4,640]{2,0,1:T(8,128)(2,1)S(1)} %bitcast.217), channel_id=1, replica_groups=mesh['group'=4,'replica'=8] {'group'}, dimensions={1} | all-to-all | bytes 2621440 | tf_op jit(solution)/shard_map/all_to_all | solution.py:279
  3933.1 173.3 %all-gather.42.cloned.1.call-done = bf16[1024,7168]{1,0:T(8,128)(2,1)} async-done(((bf16[256,7168]{1,0:T(8,128)(2,1)}), bf16[1024,7168]{1,0:T(8,128)(2,1)}) %all-gather.42.cloned.1.call-update) | async-done | bytes 14680080 | tf_op jit(solution)/shard_map/all_gather | solution.py:289
  4106.4 17.4 convolution_convert_fusion.1
  4124.1 234.4 %all-gather.44.cloned.1.call-done = bf16[1024,7168]{1,0:T(8,128)(2,1)} async-done(((bf16[256,7168]{1,0:T(8,128)(2,1)}), bf16[1024,7168]{1,0:T(8,128)(2,1)}) %all-gather.44.cloned.1.call-update) | async-done | bytes 14680080 | tf_op jit(solution)/shard_map/all_gather | solution.py:290
  4358.5 17.4 convolution_convert_fusion
  4377.1 19.9 multiply_reduce_fusion
  4399.1 8.6 psum.7
  4408.2 4.8 fusion.26
  4413.0 81.7 %reduce-scatter.31.cloned.1.call-done = f32[80,2]{1,0:T(8,128)} async-done(((f32[2560,2]{1,0:T(8,128)}), f32[80,2]{1,0:T(8,128)}) %reduce-scatter.31.cloned.1.call-update) | async-done | bytes 656
  4496.8 44.4 reduce-scatter.25.cloned.1.call-done
  4543.2 36.8 reduce-scatter.23.cloned.1.call-done
  4581.6 36.9 reduce-scatter.21.cloned.1.call-done
  4620.1 49.1 reduce-scatter.19.cloned.1.call-done
  4671.1 77.1 %reduce-scatter.33.cloned.1.call-done = bf16[80,7168]{1,0:T(8,128)(2,1)} async-done(((bf16[640,7168]{1,0:T(8,128)(2,1)}), bf16[80,7168]{1,0:T(8,128)(2,1)}) %reduce-scatter.33.cloned.1.call-update) | async-done | bytes 1146896
  4751.9 74.9 %reduce-scatter.27.cloned.1.call-done = bf16[80,7168]{1,0:T(8,128)(2,1)} async-done(((bf16[640,7168]{1,0:T(8,128)(2,1)}), bf16[80,7168]{1,0:T(8,128)(2,1)}) %reduce-scatter.27.cloned.1.call-update) | async-done | bytes 1146896 | tf_op jit(solution)/shard_map/reduce_scatter | solution.py:315
  4829.7 76.2 %reduce-scatter.29.cloned.1.call-done = bf16[80,7168]{1,0:T(8,128)(2,1)} async-done(((bf16[640,7168]{1,0:T(8,128)(2,1)}), bf16[80,7168]{1,0:T(8,128)(2,1)}) %reduce-scatter.29.cloned.1.call-update) | async-done | bytes 1146896 | tf_op jit(solution)/shard_map/reduce_scatter | solution.py:318
  (214 shorter events, 95.4 us)
Async XLA Ops:
  7.2 70.8 %all-gather.24.cloned.1.call-start = ((), (), s32[]{:S(2)}) async-start(), calls=%async_computation.15 | async-start | bytes 4096000 | tf_op jit(solution)/shard_map/all_gather | solution.py:91
  7.9 18.5 copy-start
  7.9 136.0 %all-gather.22.cloned.1.call-start = ((), (), s32[]{:S(2)}) async-start(), calls=%async_computation.14 | async-start | bytes 4096000 | tf_op jit(solution)/shard_map/all_gather | solution.py:92
  8.7 1012.9 %all-gather.50.cloned.1.call-start = ((), (), s32[]{:S(2)}) async-start(), calls=%async_computation.36 | async-start | bytes 1638400 | tf_op jit(solution)/shard_map/all_gather | solution.py:121
  24.7 1002.9 %copy-start.28 = (f32[2560]{0:T(1024)}, f32[2560]{0:T(1024)S(1)}, u32[]{:S(2)}) copy-start(f32[2560]{0:T(1024)S(1)} %reshape.535) | copy-start | bytes 30724
  25.8 1011.8 %copy-start.22 = (f32[256,80]{0,1:T(8,128)}, f32[256,80]{0,1:T(8,128)S(1)}, u32[]{:S(2)}) copy-start(f32[256,80]{0,1:T(8,128)S(1)} %get-tuple-element.147) | copy-start | bytes 245764
  25.8 1011.8 %copy-start.24 = (f32[256,80]{0,1:T(8,128)}, f32[256,80]{0,1:T(8,128)S(1)}, u32[]{:S(2)}) copy-start(f32[256,80]{0,1:T(8,128)S(1)} %get-tuple-element.148) | copy-start | bytes 245764
  27.3 1000.2 %copy-start.32 = (f32[256]{0:T(256)}, f32[256]{0:T(256)S(1)}, u32[]{:S(2)}) copy-start(f32[256]{0:T(256)S(1)} %get-tuple-element.150) | copy-start | bytes 3076
  86.8 936.9 %all-gather.48.cloned.1.call-start = ((), (), s32[]{:S(2)}) async-start(), calls=%async_computation.35 | async-start | bytes 1638400 | tf_op jit(solution)/shard_map/all_gather | solution.py:122
  147.8 879.7 %all-gather.26.cloned.1.call-start = ((), (), s32[]{:S(2)}) async-start(), calls=%async_computation.16 | async-start | bytes 16384000 | tf_op jit(solution)/shard_map/all_gather | solution.py:90
  148.4 931.0 %all-gather.28.cloned.1.call-start = ((), (), s32[]{:S(2)}) async-start(), calls=%async_computation.17 | async-start | bytes 16384000 | tf_op jit(solution)/shard_map/all_gather | solution.py:93
  149.0 1665.5 %all-gather.30.cloned.1.call-start = ((), (), s32[]{:S(2)}) async-start(), calls=%async_computation.18 | async-start | bytes 45875200 | tf_op jit(solution)/shard_map/all_gather | solution.py:170
  149.7 2279.2 %all-gather.32.cloned.1.call-start = ((), (), s32[]{:S(2)}) async-start(), calls=%async_computation.19 | async-start | bytes 45875200 | tf_op jit(solution)/shard_map/all_gather | solution.py:171
  150.5 452.2 %copy-start.37 = (s32[1,2]{1,0:T(1,128)S(1)}, s32[1,2]{1,0:T(1,128)}, u32[]{:S(2)}) copy-start(s32[1,2]{1,0:T(1,128)} %param.15) | copy-start | bytes 28
  150.5 454.0 %copy-start.36 = (bf16[640]{0:T(1024)(128)(2,1)S(1)}, bf16[640]{0:T(1024)(128)(2,1)}, u32[]{:S(2)}) copy-start(bf16[640]{0:T(1024)(128)(2,1)} %param.21) | copy-start | bytes 3844
  150.5 2893.1 %all-gather.34.cloned.1.call-start = ((), (), s32[]{:S(2)}) async-start(), calls=%async_computation.20 | async-start | bytes 45875200 | tf_op jit(solution)/shard_map/all_gather | solution.py:192
  151.2 3026.4 %reduce-scatter.17.cloned.1.call-start = ((), (), s32[]{:S(2)}) async-start(), calls=%async_computation.22 | async-start | bytes 3276800 | tf_op jit(solution)/shard_map/reduce_scatter | solution.py:255
  151.3 369.7 %collective-permute-start = (bf16[640,7168]{1,0:T(8,128)(2,1)}, bf16[640,7168]{1,0:T(8,128)(2,1)}, u32[]{:S(2)}, u32[]{:S(2)}) collective-permute-start(bf16[640,7168]{1,0:T(8,128)(2,1)} %param.22), channel_id=1, source_target_pairs={{0,8},{8,16},{16,24},{24,0},{1,9},{9,17},{17,25},{25,1},{2,10},{10... | collective-permute-start | bytes 27525128 | tf_op jit(solution)/shard_map/ppermute | solution.py:164
  521.0 505.8 %collective-permute-start.1 = (bf16[640,7168]{1,0:T(8,128)(2,1)}, bf16[640,7168]{1,0:T(8,128)(2,1)}, u32[]{:S(2)}, u32[]{:S(2)}) collective-permute-start(bf16[640,7168]{1,0:T(8,128)(2,1)} %collective-permute-done), channel_id=1, source_target_pairs={{0,8},{8,16},{16,24},{24,0},{1,9},{9,17},{17,25},{25,1},{2,10},{10... | collective-permute-start | bytes 27525128 | tf_op jit(solution)/shard_map/ppermute | solution.py:164
  1023.6 14.5 copy-start.4
  1026.8 389.3 %collective-permute-start.2 = (bf16[640,7168]{1,0:T(8,128)(2,1)}, bf16[640,7168]{1,0:T(8,128)(2,1)}, u32[]{:S(2)}, u32[]{:S(2)}) collective-permute-start(bf16[640,7168]{1,0:T(8,128)(2,1)} %collective-permute-done.1), channel_id=1, source_target_pairs={{0,8},{8,16},{16,24},{24,0},{1,9},{9,17},{17,25},{25,1},{2,10},{10... | collective-permute-start | bytes 27525128 | tf_op jit(solution)/shard_map/ppermute | solution.py:164
  1038.1 14.4 copy-start.2
  1052.5 13.1 copy-start.8
  1079.3 7.8 copy-start.26
  1087.1 1.5 copy-start.6
  1088.9 1364.8 %copy-start.12 = (bf16[256,2560]{1,0:T(8,128)(2,1)}, bf16[256,2560]{1,0:T(8,128)(2,1)S(1)}, u32[]{:S(2)}) copy-start(bf16[256,2560]{1,0:T(8,128)(2,1)S(1)} %multiply_convert_fusion.3) | copy-start | bytes 3932164
  1478.6 950.3 %copy-start.10 = (bf16[1,256,2560]{2,1,0:T(8,128)(2,1)S(1)}, bf16[1,256,2560]{2,1,0:T(8,128)(2,1)}, u32[]{:S(2)}) copy-start(bf16[1,256,2560]{2,1,0:T(8,128)(2,1)} %param.25) | copy-start | bytes 3932164
  3043.6 18.5 copy-start.7
  3062.1 20.8 copy-start.35
  3112.3 1.3 copy-start.9
  3112.3 115.4 %reduce-scatter.15.cloned.1.call-start = ((), (), s32[]{:S(2)}) async-start(), calls=%async_computation.21 | async-start | bytes 3276800 | tf_op jit(solution)/shard_map/reduce_scatter | solution.py:254
  3136.4 28.1 copy-start.3
  3176.9 50.8 %copy-start.25 = (f32[256,80]{0,1:T(8,128)S(1)}, f32[256,80]{0,1:T(8,128)}, u32[]{:S(2)}) copy-start(f32[256,80]{0,1:T(8,128)} %copy-done.24) | copy-start | bytes 245764
  3176.9 178.9 %all-gather.40.cloned.1.call-start = ((), (), s32[]{:S(2)}) async-start(), calls=%async_computation.28 | async-start | bytes 6553600 | tf_op jit(solution)/shard_map/all_gather | solution.py:286
  3177.5 51.5 %copy-start.23 = (f32[256,80]{0,1:T(8,128)S(1)}, f32[256,80]{0,1:T(8,128)}, u32[]{:S(2)}) copy-start(f32[256,80]{0,1:T(8,128)} %copy-done.22) | copy-start | bytes 245764
  3177.5 242.1 %all-gather.52.cloned.1.call-start = ((), (), s32[]{:S(2)}) async-start(), calls=%async_computation.37 | async-start | bytes 1638400 | tf_op jit(solution)/shard_map/all_gather | solution.py:285
  3179.5 268.5 %all-gather.38.cloned.1.call-start = ((), (), s32[]{:S(2)}) async-start(), calls=%async_computation.25 | async-start | bytes 1638400 | tf_op jit(solution)/shard_map/all_gather | solution.py:284
  3227.7 1.4 copy-start.21
  3228.9 1.5 copy-start.5
  3229.9 316.2 %all-gather.36.cloned.1.call-start = ((), (), s32[]{:S(2)}) async-start(), calls=%async_computation.23 | async-start | bytes 6553600 | tf_op jit(solution)/shard_map/all_gather | solution.py:283
  3241.7 584.6 %all-gather.46.cloned.1.call-start = ((), (), s32[]{:S(2)}) async-start(), calls=%async_computation.34 | async-start | bytes 18350080 | tf_op jit(solution)/shard_map/all_gather | solution.py:291
  3242.3 864.1 %all-gather.42.cloned.1.call-start = ((), (), s32[]{:S(2)}) async-start(), calls=%async_computation.30 | async-start | bytes 18350080 | tf_op jit(solution)/shard_map/all_gather | solution.py:289
  3242.9 1.3 copy-start.15
  3242.9 1115.6 %all-gather.44.cloned.1.call-start = ((), (), s32[]{:S(2)}) async-start(), calls=%async_computation.32 | async-start | bytes 18350080 | tf_op jit(solution)/shard_map/all_gather | solution.py:290
  3244.2 5.5 copy-start.16
  3245.4 110.5 %all-to-all-start.1 = ((bf16[256,4,640]{2,0,1:T(8,128)(2,1)}), bf16[256,4,640]{2,0,1:T(8,128)(2,1)}, u32[]{:S(2)}, u32[]{:S(2)}) async-start(bf16[256,4,640]{2,0,1:T(8,128)(2,1)} %bitcast.215), calls=%async_computation.6 | async-start | bytes 2621440 | tf_op jit(solution)/shard_map/all_to_all | solution.py:278
  3249.7 7.1 copy-start.20
  3249.7 1245.0 %reduce-scatter.31.cloned.1.call-start = ((), (), s32[]{:S(2)}) async-start(), calls=%async_computation.38 | async-start | bytes 1351680
  3249.8 7.1 copy-start.17
  3256.9 1.3 copy-start.1
  3256.9 2.3 copy-start.18
  3256.9 2.3 copy-start.19
  3256.9 2.3 copy-start.29
  3256.9 2.3 copy-start.33
  3263.9 1277.3 %reduce-scatter.25.cloned.1.call-start = ((), (), s32[]{:S(2)}) async-start(), calls=%async_computation.29 | async-start | bytes 3686400 | tf_op jit(solution)/shard_map/reduce_scatter | solution.py:312
  3364.1 1215.9 %reduce-scatter.23.cloned.1.call-start = ((), (), s32[]{:S(2)}) async-start(), calls=%async_computation.27 | async-start | bytes 921600 | tf_op jit(solution)/shard_map/reduce_scatter | solution.py:309
  3423.2 1195.3 %reduce-scatter.21.cloned.1.call-start = ((), (), s32[]{:S(2)}) async-start(), calls=%async_computation.26 | async-start | bytes 921600 | tf_op jit(solution)/shard_map/reduce_scatter | solution.py:306
  3451.4 1217.8 %reduce-scatter.19.cloned.1.call-start = ((), (), s32[]{:S(2)}) async-start(), calls=%async_computation.24 | async-start | bytes 3686400 | tf_op jit(solution)/shard_map/reduce_scatter | solution.py:303
  3553.9 1.5 copy-start.11
  3554.0 1194.2 %reduce-scatter.33.cloned.1.call-start = ((), (), s32[]{:S(2)}) async-start(), calls=%async_computation.39 | async-start | bytes 10321920
  3856.6 1.3 copy-start.13
  3856.7 970.2 %reduce-scatter.27.cloned.1.call-start = ((), (), s32[]{:S(2)}) async-start(), calls=%async_computation.31 | async-start | bytes 10321920 | tf_op jit(solution)/shard_map/reduce_scatter | solution.py:315
  4123.8 782.0 %reduce-scatter.29.cloned.1.call-start = ((), (), s32[]{:S(2)}) async-start(), calls=%async_computation.33 | async-start | bytes 10321920 | tf_op jit(solution)/shard_map/reduce_scatter | solution.py:318
  4377.1 31.1 copy-start.34
  (4 other events, 3.1 us)
Sparse Core Ops, SparseCore 0:
  9.6 68.3 all-gather.23
  79.5 64.2 all-gather.21
  146.0 53.1 all-gather.49
  201.3 52.9 all-gather.47
  255.7 350.3 all-gather.25
  607.5 405.5 all-gather.27
  1014.7 799.6 all-gather.29
  1816.0 612.8 all-gather.31
  2430.5 613.0 all-gather.33
  3112.4 50.8 reduce-scatter.16
  3177.1 50.6 reduce-scatter.14
  3229.1 126.7 all-gather.39
  3358.0 56.1 all-gather.51
  3416.2 31.6 all-gather.37
  3449.9 96.2 all-gather.35
  3547.6 278.6 all-gather.45
  3827.7 278.6 all-gather.41
  4107.8 250.6 all-gather.43
  4361.3 133.3 reduce-scatter.30
  4498.4 42.7 reduce-scatter.24
  4545.5 34.4 reduce-scatter.22
  4583.9 34.4 reduce-scatter.20
  4622.3 46.8 reduce-scatter.18
  4673.1 75.0 reduce-scatter.32
  4751.8 75.0 reduce-scatter.26
  4830.8 75.0 reduce-scatter.28
